TPU v7x, 128 devices: a whole 4x4x4 slice. The times are simulated.
128 devices in a mesh: gx: 4 (over y), gy: 4 (over x_lo, core), gz: 8 (over x_hi, z).
Axes of the slice: x: 4 (x_hi: 2, x_lo: 2; x = x_hi * 2 + x_lo), y: 4, z: 4, core: 2. Of those that a mesh axis runs over, the one named last changes fastest.
Arguments:
- inputs: bfloat16 [112, 112, 56, 96], P('gx', 'gy', 'gz'), may hold values from -6 to 6
- d_out: bfloat16 [112, 112, 56, 96], P('gx', 'gy', 'gz'), may hold values from -6 to 6
- layer_norm_gain: float32 [96], replicated, may hold values from 0.1 to 1.9
- layer_norm_bias: float32 [96], replicated, may hold values from -3 to 3
- w_qkv: bfloat16 [96, 288], replicated, may hold values from -0.625 to 0.625
- b_qkv: float32 [288], replicated, may hold values from -3 to 3
- w_proj: bfloat16 [96, 96], replicated, may hold values from -0.625 to 0.625
- rel_bias: float32 [3, 2197], replicated, may hold values from -4 to 240
Outputs:
- d_x: bfloat16 [112, 112, 56, 96], P('gx', 'gy', 'gz')
- g_qkv: float32 [96, 288], replicated
- g_bqkv: float32 [288], replicated
- g_proj: float32 [96, 96], replicated
- g_rel: float32 [3, 2197], replicated
- gain_gradient: float32 [96], replicated
- g_shift: float32 [96], replicated
All inputs are finite; a program needn't handle non-finite values.
Results may differ from a plain program's by a relative error of at most 0.011.
Values may be sent and summed in bfloat16 or wider, within the bound.
A program may use at most 192 MiB of HBM per device.

v0:
```python
import jax
import jax.numpy as jnp
from jax import lax
from jax.sharding import PartitionSpec as P

WIN = 7
SHIFT = 3


def shifted(block, axis, distance):
    devices = range(lax.axis_size(axis))
    route = [((i - distance) % len(devices), i) for i in devices]
    return lax.ppermute(block, axis, route)


def in_one(arrays, axis):
    ends = [0]
    for a in arrays:
        ends.append(ends[-1] + a.size)
    so_far = lax.psum(jnp.concatenate([a.ravel() for a in arrays]), axis)
    return tuple((so_far[b:e].reshape(a.shape) for a, b, e in zip(arrays, ends, ends[1:])))


def offset_ones(span):
    first = jnp.arange(span)[:, None, None]
    second = jnp.arange(span)[None, :, None]
    third = jnp.arange(2 * span - 1)[None, None, :]
    return (first - second + span - 1 == third).astype(jnp.float32)


def expand_table(table, span):
    exact = lax.Precision.HIGHEST
    ones = offset_ones(span)
    width = 2 * span - 1
    heads = table.shape[0]
    cube = table.reshape(heads, width, width, width)
    section = jnp.einsum("hxyz,cCz->hxycC", cube, ones, precision=exact)
    section = jnp.einsum("hxycC,bBy->hxbcBC", section, ones, precision=exact)
    section = jnp.einsum("hxbcBC,aAx->habcABC", section, ones, precision=exact)
    return section.reshape(heads, span**3, span**3)


def fold_table(pairs, span):
    exact = lax.Precision.HIGHEST
    ones = offset_ones(span)
    heads = pairs.shape[0]
    grid = pairs.reshape(heads, span, span, span, span, span, span)
    section = jnp.einsum("habcABC,aAx->hxbcBC", grid, ones, precision=exact)
    section = jnp.einsum("hxbcBC,bBy->hxycC", section, ones, precision=exact)
    section = jnp.einsum("hxycC,cCz->hxyz", section, ones, precision=exact)
    return section.reshape(heads, -1)


def region_label(start, cells, count):
    places = start + jnp.arange(cells)
    return jnp.where(places < count - WIN, 0, jnp.where(places < count - SHIFT, 1, 2)).astype(
        jnp.int32
    )


def to_windows(array):
    first, second, third = array.shape[:3]
    rest = array.shape[3:]
    shaped = array.reshape((first // WIN, WIN, second // WIN, WIN, third // WIN, WIN) + rest)
    order = (0, 2, 4, 1, 3, 5) + tuple(range(6, 6 + len(rest)))
    return shaped.transpose(order).reshape((-1, WIN**3) + rest)


def from_windows(array, first, second, third):
    feats = array.shape[-1]
    shaped = array.reshape(first // WIN, second // WIN, third // WIN, WIN, WIN, WIN, feats)
    return shaped.transpose(0, 3, 1, 4, 2, 5, 6).reshape(first, second, third, feats)


def forward_depth(pair):
    arrived = shifted(pair[:, :SHIFT], "gx", -1)
    return jnp.concatenate([pair[:, SHIFT:], arrived], 1)


def forward_height(pair):
    arrived = shifted(pair[:, :, :SHIFT], "gy", -1)
    return jnp.concatenate([pair[:, :, SHIFT:], arrived], 2)


def forward_width(pair):
    arrived = shifted(pair[:, :, :, :SHIFT], "gz", -1)
    return jnp.concatenate([pair[:, :, :, SHIFT:], arrived], 3)


def backward_depth(field):
    edge = field.shape[0] - SHIFT
    arrived = shifted(field[edge:], "gx", 1)
    return jnp.concatenate([arrived, field[:edge]], 0)


def backward_height(field):
    edge = field.shape[1] - SHIFT
    arrived = shifted(field[:, edge:], "gy", 1)
    return jnp.concatenate([arrived, field[:, :edge]], 1)


def backward_width(field):
    edge = field.shape[2] - SHIFT
    arrived = shifted(field[:, :, edge:], "gz", 1)
    return jnp.concatenate([arrived, field[:, :, :edge]], 2)


def window_pass(ln_w, dy_w, lab_w, w_qkv, b_qkv, w_proj, bias_full):
    f32 = jnp.float32
    bf16 = jnp.bfloat16
    group, tok, feats = ln_w.shape
    heads = bias_full.shape[0]
    hdim = feats // heads
    scale = hdim ** (-0.5)
    qkv = jnp.einsum("gtc,cf->gtf", ln_w, w_qkv, preferred_element_type=f32) + b_qkv
    qkv = qkv.astype(bf16).reshape(group, tok, 3, heads, hdim)
    query = qkv[:, :, 0].transpose(0, 2, 1, 3)
    keys = qkv[:, :, 1].transpose(0, 2, 1, 3)
    values = qkv[:, :, 2].transpose(0, 2, 1, 3)
    scores = (
        jnp.einsum("ghid,ghjd->ghij", query, keys, preferred_element_type=f32) * scale
        + bias_full[None]
    )
    allowed = (lab_w[:, :, None] == lab_w[:, None, :])[:, None]
    scores = jnp.where(allowed, scores, f32(-1e30))
    top = jnp.max(scores, -1, keepdims=True)
    expo = jnp.exp(scores - top)
    probs = expo / jnp.sum(expo, -1, keepdims=True)
    probs_b = probs.astype(bf16)
    attended = jnp.einsum("ghij,ghjd->ghid", probs_b, values, preferred_element_type=f32)
    attended = attended.transpose(0, 2, 1, 3).reshape(group, tok, feats).astype(bf16)
    grad_att = jnp.einsum("gtc,fc->gtf", dy_w, w_proj, preferred_element_type=f32).astype(bf16)
    proj_part = jnp.einsum("gtf,gtc->fc", attended, dy_w, preferred_element_type=f32)
    grad_heads = grad_att.reshape(group, tok, heads, hdim).transpose(0, 2, 1, 3)
    grad_probs = jnp.einsum("ghid,ghjd->ghij", grad_heads, values, preferred_element_type=f32)
    grad_v = jnp.einsum("ghij,ghid->ghjd", probs_b, grad_heads, preferred_element_type=f32)
    grad_scores = probs * (grad_probs - jnp.sum(probs * grad_probs, -1, keepdims=True))
    rel_part = jnp.sum(grad_scores, 0)
    scores_b = grad_scores.astype(bf16)
    grad_q = jnp.einsum("ghij,ghjd->ghid", scores_b, keys, preferred_element_type=f32) * scale
    grad_k = jnp.einsum("ghij,ghid->ghjd", scores_b, query, preferred_element_type=f32) * scale
    grad_qkv = (
        jnp.stack([grad_q, grad_k, grad_v], 1)
        .transpose(0, 3, 1, 2, 4)
        .reshape(group, tok, 3 * feats)
    )
    bias_part = jnp.sum(grad_qkv, (0, 1))
    qkv_b = grad_qkv.astype(bf16)
    weight_part = jnp.einsum("gtc,gtf->cf", ln_w, qkv_b, preferred_element_type=f32)
    grad_in = jnp.einsum("gtf,cf->gtc", qkv_b, w_qkv, preferred_element_type=f32)
    return (grad_in, (weight_part, bias_part, proj_part, rel_part))


def shards(inputs, d_out, layer_norm_gain, layer_norm_bias, w_qkv, b_qkv, w_proj, rel_bias):
    f32 = jnp.float32
    cells_x, cells_y, cells_z, feats = inputs.shape
    tok = WIN**3
    heads = rel_bias.shape[0]
    xf = inputs.astype(f32)
    centered_input = xf - jnp.mean(xf, -1, keepdims=True)
    inverse_deviation = lax.rsqrt(
        jnp.mean(centered_input * centered_input, -1, keepdims=True) + 1e-05
    )
    normalized_input = centered_input * inverse_deviation
    normalized_tokens = (normalized_input * layer_norm_gain + layer_norm_bias).astype(jnp.bfloat16)
    moved_pair = jnp.stack([normalized_tokens, d_out])
    forward_steps = (forward_depth, forward_height, forward_width)
    backward_steps = (backward_depth, backward_height, backward_width)
    for advance in forward_steps:
        moved_pair = advance(moved_pair)
    label_x = region_label(lax.axis_index("gx") * cells_x, cells_x, cells_x * lax.axis_size("gx"))
    label_y = region_label(lax.axis_index("gy") * cells_y, cells_y, cells_y * lax.axis_size("gy"))
    label_z = region_label(lax.axis_index("gz") * cells_z, cells_z, cells_z * lax.axis_size("gz"))
    labels = label_x[:, None, None] * 9 + label_y[None, :, None] * 3 + label_z[None, None, :]
    bias_full = expand_table(rel_bias, WIN)
    group = cells_y // WIN * (cells_z // WIN)
    win_ln = to_windows(moved_pair[0]).reshape(-1, group, tok, feats)
    win_dy = to_windows(moved_pair[1]).reshape(-1, group, tok, feats)
    win_lab = to_windows(labels).reshape(-1, group, tok)

    def step(carry, item):
        grad_in, parts = window_pass(item[0], item[1], item[2], w_qkv, b_qkv, w_proj, bias_full)
        return (tuple((total + part for total, part in zip(carry, parts))), grad_in)

    start = (
        jnp.zeros((feats, 3 * feats), f32),
        jnp.zeros((3 * feats,), f32),
        jnp.zeros((feats, feats), f32),
        jnp.zeros((heads, tok, tok), f32),
    )
    sums, grad_win = lax.scan(step, start, (win_ln, win_dy, win_lab))
    normalized_output_gradient = from_windows(
        grad_win.reshape(-1, tok, feats), cells_x, cells_y, cells_z
    )
    for retreat in backward_steps:
        normalized_output_gradient = retreat(normalized_output_gradient)
    normalized_gradient = normalized_output_gradient * layer_norm_gain
    input_gradient_norm = inverse_deviation * (
        normalized_gradient
        - jnp.mean(normalized_gradient, -1, keepdims=True)
        - normalized_input * jnp.mean(normalized_gradient * normalized_input, -1, keepdims=True)
    )
    d_x = (d_out.astype(f32) + input_gradient_norm).astype(jnp.bfloat16)
    rel_local = fold_table(sums[3], WIN)
    local_gain = jnp.sum(normalized_output_gradient * normalized_input, (0, 1, 2))
    shift_local = jnp.sum(normalized_output_gradient, (0, 1, 2))
    totals = in_one(
        (sums[0], sums[1], sums[2], rel_local, local_gain, shift_local), ("gx", "gy", "gz")
    )
    count = (
        cells_x
        * cells_y
        * cells_z
        * lax.axis_size("gx")
        * lax.axis_size("gy")
        * lax.axis_size("gz")
    )
    inverse_width_factor = float(count) ** (-0.5)
    return (
        d_x,
        totals[0] * inverse_width_factor,
        totals[1] * inverse_width_factor,
        totals[2] * inverse_width_factor,
        totals[3] * inverse_width_factor,
        totals[4] * inverse_width_factor,
        totals[5] * inverse_width_factor,
    )


def solution(mesh):
    placed = (P("gx", "gy", "gz", None), P("gx", "gy", "gz", None), P(), P(), P(), P(), P(), P())
    return jax.shard_map(
        shards,
        mesh=mesh,
        in_specs=placed,
        out_specs=(P("gx", "gy", "gz", None), P(), P(), P(), P(), P(), P()),
        check_vma=False,
    )
```

profile of v0, /device:TPU:1, one launch (start us, length us, event | category | flops | bytes accessed | tf_op | source)
XLA Modules:
  0.0 693.7 jit_solution(11061455618265051562)
XLA Ops:
  7.2 2.4 convert_reduce_fusion
  15.1 3.6 collective-permute-start
  20.4 9.5 %convolution_bitcast_fusion.5 = f32[3,13,7,7,7,7]{1,2,5,3,0,4:T(8,128)S(1)} fusion(f32[3,13,13,7,7]{2,3,1,0,4:T(8,128)S(1)} %convolution_bitcast_fusion.7, s32[7,7]{0,1:T(8,128)S(1)} %subtract_add_fusion), kind=kOutput, calls=%fused_computation.96 | convolution fusion | flops 14608321 | bytes 474124 | tf_op jit(solution)/shard_map/hxycC,bBy->hxbcBC/dot_general | solution.py:38
  30.9 18.5 %collective-permute-start.1 = (bf16[2,28,3,7,96]{4,3,2,1,0:T(8,128)(2,1)S(1)}, bf16[2,28,3,7,96]{4,3,2,1,0:T(8,128)(2,1)S(1)}, u32[]{:S(2)}, u32[]{:S(2)}) collective-permute-start(bf16[2,28,3,7,96]{4,3,2,1,0:T(8,128)(2,1)S(1)} %pad_maximum_fusion.5), channel_id=1, source_target_pairs={{8,0},{16,8},{24,16},{0,24},{9,1},{17,9},{25,17},{1,25},{10,2},{18... | collective-permute-start | bytes 677384 | tf_op jit(solution)/shard_map/ppermute | solution.py:13
  50.3 5.2 collective-permute-done.1
  56.3 2.9 copy.74
  59.2 5.9 collective-permute-start.2
  65.2 71.1 %convolution_bitcast_fusion.3 = f32[3,7,7,7,7,7,7]{6,4,5,3,2,0,1:T(8,128)} fusion(f32[3,13,7,7,7,7]{1,2,5,3,0,4:T(8,128)S(1)} %convolution_bitcast_fusion.5, pred[7,7,13,1,1,1,1]{2,0,1,6,5,4,3:T(8,128)(4,1)S(1)} %fusion.73), kind=kOutput, calls=%fused_computation.61 | convolution fusion | flops 55059736 | bytes 1786981 | tf_op jit(solution)/shard_map/hxbcBC,aAx->habcABC/dot_general | solution.py:39
  136.3 59.5 %copy.82 = f32[3,7,7,7,7,7,7]{3,2,1,6,5,4,0:T(8,128)} copy(f32[3,7,7,7,7,7,7]{6,4,5,3,2,0,1:T(8,128)} %convolution_bitcast_fusion.3) | data formatting | bytes 2823576
  195.9 21.0 %add.230 = f32[3,343,343]{1,2,0:T(8,128)} reshape(f32[3,7,7,7,7,7,7]{3,2,1,6,5,4,0:T(8,128)} %copy.82) | data formatting | bytes 2823576 | tf_op jit(solution)/shard_map/while/body/eval_jaxpr/add | solution.py:121
  217.9 2.6 fusion.67
  226.2 2.5 copy.81
  230.6 2.5 copy.83
  233.2 134.0 %while.20 = (s32[]{:T(128)}, f32[96,288]{1,0:T(8,128)}, f32[288]{0:T(512)S(1)}, f32[96,96]{1,0:T(8,128)S(1)}, f32[3,343,343]{1,2,0:T(8,128)}, /*index=5*/f32[4,4...) while((s32[]{:T(128)}, f32[96,288]{1,0:T(8,128)}, ...), condition=%wide.wide.region_8.9_spmd.clone, body=%wide.wide.region_2.8_spmd.clone.sunk | while | flops 848489408 | bytes 107633568 | solution.py:191
  235.7 7.0 %fusion.174 = (f32[4,3,343]{2,1,0:T(4,128)S(1)}, f32[4,3,343,343]{2,3,1,0:T(8,128)}) fusion(f32[3,343,343]{1,2,0:T(8,128)} %get-tuple-element.420, pred[4,343,343]{1,2,0:T(8,128)(4,1)} %broadcast_compare_fusion.3, bf16[4,343,3,3,32]{1,4,3,2,0:T(8,128)(2,1)S(1)} %bitcast.281), kind=kOutput, calls=%fused_computation.146.clone.clone.1 | convolution fusion | flops 97413720 | bytes 8135824 | tf_op jit(solution)/shard_map/while/body/eval_jaxpr/sub | solution.py:127
  243.0 6.9 multiply_reduce_fusion.4
  249.9 4.2 fusion.176
  258.5 2.1 fusion.180
  261.9 3.6 fusion.182
  268.1 7.0 %fusion.174 = (f32[4,3,343]{2,1,0:T(4,128)S(1)}, f32[4,3,343,343]{2,3,1,0:T(8,128)}) fusion(f32[3,343,343]{1,2,0:T(8,128)} %get-tuple-element.420, pred[4,343,343]{1,2,0:T(8,128)(4,1)} %broadcast_compare_fusion.3, bf16[4,343,3,3,32]{1,4,3,2,0:T(8,128)(2,1)S(1)} %bitcast.281), kind=kOutput, calls=%fused_computation.146.clone.clone.1 | convolution fusion | flops 97413720 | bytes 8135824 | tf_op jit(solution)/shard_map/while/body/eval_jaxpr/sub | solution.py:127
  275.3 6.9 multiply_reduce_fusion.4
  282.2 4.2 fusion.176
  290.8 2.1 fusion.180
  292.9 2.7 select_add_fusion.7
  295.7 3.6 fusion.182
  301.9 7.0 %fusion.174 = (f32[4,3,343]{2,1,0:T(4,128)S(1)}, f32[4,3,343,343]{2,3,1,0:T(8,128)}) fusion(f32[3,343,343]{1,2,0:T(8,128)} %get-tuple-element.420, pred[4,343,343]{1,2,0:T(8,128)(4,1)} %broadcast_compare_fusion.3, bf16[4,343,3,3,32]{1,4,3,2,0:T(8,128)(2,1)S(1)} %bitcast.281), kind=kOutput, calls=%fused_computation.146.clone.clone.1 | convolution fusion | flops 97413720 | bytes 8135824 | tf_op jit(solution)/shard_map/while/body/eval_jaxpr/sub | solution.py:127
  309.1 6.9 multiply_reduce_fusion.4
  316.1 4.2 fusion.176
  324.6 2.1 fusion.180
  326.8 2.7 select_add_fusion.7
  329.5 3.6 fusion.182
  335.7 6.9 %fusion.174 = (f32[4,3,343]{2,1,0:T(4,128)S(1)}, f32[4,3,343,343]{2,3,1,0:T(8,128)}) fusion(f32[3,343,343]{1,2,0:T(8,128)} %get-tuple-element.420, pred[4,343,343]{1,2,0:T(8,128)(4,1)} %broadcast_compare_fusion.3, bf16[4,343,3,3,32]{1,4,3,2,0:T(8,128)(2,1)S(1)} %bitcast.281), kind=kOutput, calls=%fused_computation.146.clone.clone.1 | convolution fusion | flops 97413720 | bytes 8135824 | tf_op jit(solution)/shard_map/while/body/eval_jaxpr/sub | solution.py:127
  342.9 6.9 multiply_reduce_fusion.4
  349.9 4.2 fusion.176
  358.4 2.1 fusion.180
  360.6 2.7 select_add_fusion.7
  363.3 3.6 fusion.182
  367.1 3.4 copy.84
  373.5 20.0 %reshape.174 = f32[3,7,7,7,7,7,7]{3,2,1,6,5,4,0:T(8,128)} reshape(f32[3,343,343]{1,2,0:T(8,128)S(1)} %copy-done) | data formatting | bytes 2823576 | tf_op jit(solution)/shard_map/reshape | solution.py:47
  393.5 59.7 %copy.88 = f32[3,7,7,7,7,7,7]{1,6,4,5,3,2,0:T(8,128)} copy(f32[3,7,7,7,7,7,7]{3,2,1,6,5,4,0:T(8,128)} %reshape.174) | data formatting | bytes 2823576 | tf_op jit(solution)/shard_map/reshape | solution.py:47
  454.0 25.1 %convolution_bitcast_fusion.4 = f32[3,13,7,7,7,7]{1,5,4,3,2,0:T(8,128)} fusion(f32[3,7,7,7,7,7,7]{1,6,4,5,3,2,0:T(8,128)} %copy.88, s32[7,7]{0,1:T(8,128)S(1)} %copy-done.23), kind=kOutput, calls=%fused_computation.95 | convolution fusion | flops 55060372 | bytes 1786540 | tf_op jit(solution)/shard_map/habcABC,aAx->hxbcBC/dot_general | solution.py:48
  479.1 12.7 %copy.89 = f32[3,13,7,7,7,7]{2,3,4,5,1,0:T(8,128)} copy(f32[3,13,7,7,7,7]{1,5,4,3,2,0:T(8,128)} %convolution_bitcast_fusion.4) | data formatting | bytes 749112 | tf_op jit(solution)/shard_map/habcABC,aAx->hxbcBC/transpose | solution.py:48
  496.7 5.4 convolution_bitcast_fusion.6
  503.7 4.0 slice_reduce_fusion
  507.6 22.6 %collective-permute-done.5 = f32[28,28,3,96]{3,1,2,0:T(8,128)S(1)} collective-permute-done((f32[28,28,3,96]{3,1,2,0:T(8,128)}, f32[28,28,3,96]{3,1,2,0:T(8,128)S(1)}, u32[]{:S(2)}, u32[]{:S(2)}) %collective-permute-start.5) | collective-permute-done | bytes 903200 | tf_op jit(solution)/shard_map/ppermute | solution.py:13
  532.0 6.0 fusion.61
  540.9 8.0 %fusion.60 = bf16[28,28,7,96]{3,2,1,0:T(8,128)(2,1)} fusion(bf16[28,28,7,96]{3,2,1,0:T(8,128)(2,1)S(1)} %copy-done.2, bf16[28,28,7,96]{3,2,1,0:T(8,128)(2,1)S(1)} %copy-done.6, f32[28,28,7]{2,1,0:T(8,128)S(1)} %broadcast_multiply_fusion, f32[28,28,7]{2,1,0:T(8,128)S(1)} %broadcast_multiply_fusion.1, f32[96]{0:T(128)S(1)} %copy-done.27, ...), kind=kLoop, calls=%fused_computation.78 | loop fusion | flops 6322176 | bytes 5356672 | tf_op jit(solution)/shard_map/convert_element_type | solution.py:203
  548.9 130.4 %all-reduce.2.cloned.1.call-done = f32[43935]{0:T(1024)} async-done(((f32[43935]{0:T(1024)}), f32[43935]{0:T(1024)}) %all-reduce.2.cloned.1.call-update) | async-done | bytes 175756 | tf_op jit(solution)/shard_map/psum | solution.py:20
  (220 shorter events, 70.4 us)
Async XLA Ops:
  7.2 4.6 copy-start.26
  7.2 4.6 copy-start.28
  7.2 672.1 %all-reduce.2.cloned.1.call-start = ((), (), s32[]{:S(2)}) async-start(), calls=%async_computation | async-start | bytes 352256 | tf_op jit(solution)/shard_map/psum | solution.py:20
  9.8 4.1 copy-start.16
  9.8 5.2 copy-start.5
  13.8 4.9 copy-start.25
  15.1 15.7 %collective-permute-start = (bf16[2,3,28,7,96]{4,3,2,1,0:T(8,128)(2,1)S(1)}, bf16[2,3,28,7,96]{4,3,2,1,0:T(8,128)(2,1)S(1)}, u32[]{:S(2)}, u32[]{:S(2)}) collective-permute-start(bf16[2,3,28,7,96]{4,3,2,1,0:T(8,128)(2,1)S(1)} %pad_maximum_fusion.6), channel_id=1, source_target_pairs={{32,0},{64,32},{96,64},{0,96},{33,1},{65,33},{97,65},{1,97},{34,2}... | collective-permute-start | bytes 677384 | tf_op jit(solution)/shard_map/ppermute | solution.py:13
  18.7 30.7 %copy-start.22 = (s32[7,7]{0,1:T(8,128)}, s32[7,7]{0,1:T(8,128)S(1)}, u32[]{:S(2)}) copy-start(s32[7,7]{0,1:T(8,128)S(1)} %subtract_add_fusion) | copy-start | bytes 592
  19.0 11.0 %copy-start.12 = (bf16[1,28,28,7,96]{4,3,2,1,0:T(8,128)(2,1)S(1)}, bf16[1,28,28,7,96]{4,3,2,1,0:T(8,128)(2,1)}, u32[]{:S(2)}) copy-start(bf16[1,28,28,7,96]{4,3,2,1,0:T(8,128)(2,1)} %copy-done.11) | copy-start | bytes 3161092
  30.9 24.6 %collective-permute-start.1 = (bf16[2,28,3,7,96]{4,3,2,1,0:T(8,128)(2,1)S(1)}, bf16[2,28,3,7,96]{4,3,2,1,0:T(8,128)(2,1)S(1)}, u32[]{:S(2)}, u32[]{:S(2)}) collective-permute-start(bf16[2,28,3,7,96]{4,3,2,1,0:T(8,128)(2,1)S(1)} %pad_maximum_fusion.5), channel_id=1, source_target_pairs={{8,0},{16,8},{24,16},{0,24},{9,1},{17,9},{25,17},{1,25},{10,2},{18... | collective-permute-start | bytes 677384 | tf_op jit(solution)/shard_map/ppermute | solution.py:13
  55.5 3.7 copy-start.20
  59.2 161.3 %collective-permute-start.2 = (bf16[2,28,28,3,96]{4,0,3,2,1:T(2,128)(2,1)}, bf16[2,28,28,3,96]{4,0,3,2,1:T(2,128)(2,1)}, u32[]{:S(2)}, u32[]{:S(2)}) collective-permute-start(bf16[2,28,28,3,96]{4,0,3,2,1:T(2,128)(2,1)} %copy.74), channel_id=1, source_target_pairs={{1,0},{2,1},{3,2},{4,3},{5,4},{6,5},{7,6},{0,7},{9,8},{10,9},{11,1... | collective-permute-start | bytes 2709512 | tf_op jit(solution)/shard_map/ppermute | solution.py:13
  228.7 4.4 copy-start.17
  228.7 4.4 copy-start.21
  228.7 4.4 copy-start.24
  233.3 9.3 %copy-start.9 = (bf16[4,4,343,96]{2,3,1,0:T(8,128)(2,1)}, bf16[4,4,343,96]{2,3,1,0:T(8,128)(2,1)S(1)}, u32[]{:S(2)}) copy-start(bf16[4,4,343,96]{2,3,1,0:T(8,128)(2,1)S(1)} %get-tuple-element.413) | copy-start | bytes 3161092 | tf_op jit(solution)/shard_map/while
  233.4 9.3 %copy-start.13 = (bf16[4,4,343,96]{2,3,1,0:T(8,128)(2,1)}, bf16[4,4,343,96]{2,3,1,0:T(8,128)(2,1)S(1)}, u32[]{:S(2)}) copy-start(bf16[4,4,343,96]{2,3,1,0:T(8,128)(2,1)S(1)} %get-tuple-element.418) | copy-start | bytes 3161092 | tf_op jit(solution)/shard_map/while
  242.9 6.9 slice-start
  242.9 6.9 slice-start.1
  261.8 3.6 copy-start.14
  261.8 3.8 copy-start.10
  265.7 9.3 %copy-start.9 = (bf16[4,4,343,96]{2,3,1,0:T(8,128)(2,1)}, bf16[4,4,343,96]{2,3,1,0:T(8,128)(2,1)S(1)}, u32[]{:S(2)}) copy-start(bf16[4,4,343,96]{2,3,1,0:T(8,128)(2,1)S(1)} %get-tuple-element.413) | copy-start | bytes 3161092 | tf_op jit(solution)/shard_map/while
  265.7 9.3 %copy-start.13 = (bf16[4,4,343,96]{2,3,1,0:T(8,128)(2,1)}, bf16[4,4,343,96]{2,3,1,0:T(8,128)(2,1)S(1)}, u32[]{:S(2)}) copy-start(bf16[4,4,343,96]{2,3,1,0:T(8,128)(2,1)S(1)} %get-tuple-element.418) | copy-start | bytes 3161092 | tf_op jit(solution)/shard_map/while
  275.3 6.9 slice-start
  275.3 6.9 slice-start.1
  295.7 3.8 copy-start.10
  299.5 9.3 %copy-start.9 = (bf16[4,4,343,96]{2,3,1,0:T(8,128)(2,1)}, bf16[4,4,343,96]{2,3,1,0:T(8,128)(2,1)S(1)}, u32[]{:S(2)}) copy-start(bf16[4,4,343,96]{2,3,1,0:T(8,128)(2,1)S(1)} %get-tuple-element.413) | copy-start | bytes 3161092 | tf_op jit(solution)/shard_map/while
  299.5 9.3 %copy-start.13 = (bf16[4,4,343,96]{2,3,1,0:T(8,128)(2,1)}, bf16[4,4,343,96]{2,3,1,0:T(8,128)(2,1)S(1)}, u32[]{:S(2)}) copy-start(bf16[4,4,343,96]{2,3,1,0:T(8,128)(2,1)S(1)} %get-tuple-element.418) | copy-start | bytes 3161092 | tf_op jit(solution)/shard_map/while
  309.1 6.9 slice-start
  309.1 6.9 slice-start.1
  329.5 3.6 copy-start.14
  329.5 3.8 copy-start.10
  333.3 9.3 %copy-start.9 = (bf16[4,4,343,96]{2,3,1,0:T(8,128)(2,1)}, bf16[4,4,343,96]{2,3,1,0:T(8,128)(2,1)S(1)}, u32[]{:S(2)}) copy-start(bf16[4,4,343,96]{2,3,1,0:T(8,128)(2,1)S(1)} %get-tuple-element.413) | copy-start | bytes 3161092 | tf_op jit(solution)/shard_map/while
  333.4 9.3 %copy-start.13 = (bf16[4,4,343,96]{2,3,1,0:T(8,128)(2,1)}, bf16[4,4,343,96]{2,3,1,0:T(8,128)(2,1)S(1)}, u32[]{:S(2)}) copy-start(bf16[4,4,343,96]{2,3,1,0:T(8,128)(2,1)S(1)} %get-tuple-element.418) | copy-start | bytes 3161092 | tf_op jit(solution)/shard_map/while
  342.9 6.9 slice-start
  342.9 6.9 slice-start.1
  363.3 3.8 copy-start.10
  371.7 81.5 %collective-permute-start.3 = (f32[3,28,7,96]{3,2,1,0:T(8,128)}, f32[3,28,7,96]{3,2,1,0:T(8,128)S(1)}, u32[]{:S(2)}, u32[]{:S(2)}) collective-permute-start(f32[3,28,7,96]{3,2,1,0:T(8,128)} %slice.103), channel_id=1, source_target_pairs={{96,0},{0,32},{32,64},{64,96},{97,1},{1,33},{33,65},{65,97},{98,2}... | collective-permute-start | bytes 677384 | tf_op jit(solution)/shard_map/ppermute | solution.py:13
  393.5 59.7 %copy-start.4 = (f32[25,28,7,96]{3,2,1,0:T(8,128)S(1)}, f32[25,28,7,96]{3,2,1,0:T(8,128)}, u32[]{:S(2)}) copy-start(f32[25,28,7,96]{3,2,1,0:T(8,128)} %slice.104) | copy-start | bytes 5644804
  454.0 37.7 %collective-permute-start.4 = (f32[28,3,7,96]{3,2,1,0:T(8,128)}, f32[28,3,7,96]{3,2,1,0:T(8,128)}, u32[]{:S(2)}, u32[]{:S(2)}) collective-permute-start(f32[28,3,7,96]{3,2,1,0:T(8,128)} %pad_maximum_fusion.4), channel_id=1, source_target_pairs={{24,0},{0,8},{8,16},{16,24},{25,1},{1,9},{9,17},{17,25},{26,2},{2,... | collective-permute-start | bytes 677384 | tf_op jit(solution)/shard_map/ppermute | solution.py:13
  491.7 5.0 copy-start.3
  493.3 8.8 %copy-start.15 = (f32[28,28,7,96]{3,2,1,0:T(8,128)}, f32[28,28,7,96]{3,2,1,0:T(8,128)S(1)}, u32[]{:S(2)}) copy-start(f32[28,28,7,96]{3,2,1,0:T(8,128)S(1)} %fusion.63) | copy-start | bytes 6322180
  495.0 8.4 %copy-start.19 = (f32[96,288]{1,0:T(8,128)S(1)}, f32[96,288]{1,0:T(8,128)}, u32[]{:S(2)}) copy-start(f32[96,288]{1,0:T(8,128)} %get-tuple-element.79) | copy-start | bytes 331780
  495.0 35.2 %collective-permute-start.5 = (f32[28,28,3,96]{3,1,2,0:T(8,128)}, f32[28,28,3,96]{3,1,2,0:T(8,128)S(1)}, u32[]{:S(2)}, u32[]{:S(2)}) collective-permute-start(f32[28,28,3,96]{3,1,2,0:T(8,128)} %copy.86), channel_id=1, source_target_pairs={{7,0},{0,1},{1,2},{2,3},{3,4},{4,5},{5,6},{6,7},{15,8},{8,9},{9,10... | collective-permute-start | bytes 2709512 | tf_op jit(solution)/shard_map/ppermute | solution.py:13
  503.6 27.9 %copy-start.2 = (bf16[28,28,7,96]{3,2,1,0:T(8,128)(2,1)S(1)}, bf16[28,28,7,96]{3,2,1,0:T(8,128)(2,1)}, u32[]{:S(2)}) copy-start(bf16[28,28,7,96]{3,2,1,0:T(8,128)(2,1)} %param.10) | copy-start | bytes 3161092
  503.6 27.9 %copy-start.27 = (f32[96]{0:T(128)S(1)}, f32[96]{0:T(128)}, u32[]{:S(2)}) copy-start(f32[96]{0:T(128)} %param.12) | copy-start | bytes 1156
  531.5 6.4 copy-start.8
  532.0 8.9 %copy-start.6 = (bf16[28,28,7,96]{3,2,1,0:T(8,128)(2,1)S(1)}, bf16[28,28,7,96]{3,2,1,0:T(8,128)(2,1)}, u32[]{:S(2)}) copy-start(bf16[28,28,7,96]{3,2,1,0:T(8,128)(2,1)} %param.11) | copy-start | bytes 3161092
  (8 other events, 18.9 us)
Sparse Core Ops, SparseCore 0:
  538.9 140.4 all-reduce.1
where the time goes:
time: 702 us; the launch traced here: 694 us
  matrix products  211 us (30%)
  local copies, waits for them, and re-layouts  207 us (29%)
  waiting for transfers between devices  158 us (23%)
  other arithmetic  74.5 us (11%)
  starting transfers between devices  28.3 us (4%)
  between operations  14.8 us (2%)
    psum x1, waiting for transfers between devices, in_one(): so_far = lax.psum(jnp.concatenate([a.ravel() for a in arrays]), axis)  130 us
    reshape x2, local copies, waits for them, and re-layouts, fold_table(): grid = pairs.reshape(heads, span, span, span, span, span, span)  79.7 us
    dot_general x1, matrix products, expand_table(): section = jnp.einsum('hxbcBC,aAx->habcABC', section, ones, precision=exact)  71.1 us
    unnamed x53, local copies, waits for them, and re-layouts  67.9 us
    ppermute x6, starting transfers between devices, shifted(): return lax.ppermute(block, axis, route)  28.3 us
    sub x4, matrix products, window_pass(): expo = jnp.exp(scores - top)  27.8 us
    ppermute x6, waiting for transfers between devices, shifted(): return lax.ppermute(block, axis, route)  27.8 us
    dot_general x4, matrix products, window_pass(): jnp.einsum('ghid,ghjd->ghij', grad_heads, values, preferred_element_type=...  27.7 us
  transfers between devices with their start and end apart: 7, of which 3 were waited for; matrix products, arithmetic and copies ran while one was open for 44% of the time, Pallas kernels for 0%

commit v1 on v0

--- a/solution.py
+++ b/solution.py
@@ -17,7 +17,13 @@
     ends = [0]
     for a in arrays:
         ends.append(ends[-1] + a.size)
-    so_far = lax.psum(jnp.concatenate([a.ravel() for a in arrays]), axis)
+
+    def handle_heads_up(page, link_axis):
+        all_values = lax.all_gather(page, link_axis)
+        near = jnp.sum(all_values, axis=0)
+        return near
+
+    so_far = handle_heads_up(jnp.concatenate([a.ravel() for a in arrays]), axis)
     return tuple((so_far[b:e].reshape(a.shape) for a, b, e in zip(arrays, ends, ends[1:])))
 
 

time: 702 us -> 832 us (1.19)
  waiting for transfers between devices: 158 us -> 244 us
  local copies, waits for them, and re-layouts: 207 us -> 248 us
    unnamed x1 -> x2, waiting for transfers between devices: 0.02 us -> 214 us
    psum x1 -> x0, waiting for transfers between devices: 130 us -> none  [in_one(): so_far = lax.psum(jnp.concatenate([a.ravel() for a in arrays]), axis)]
    all_gather x0 -> x1, local copies, waits for them, and re-layouts: none -> 27.6 us  [handle_heads_up(): all_values = lax.all_gather(page, link_axis)]
    unnamed x53 -> x63, local copies, waits for them, and re-layouts: 67.9 us -> 79.1 us
    reduce_sum x0 -> x1, other arithmetic: none -> 8.48 us  [handle_heads_up(): near = jnp.sum(all_values, axis=0)]
  transfers between devices with their start and end apart: 7 -> 7, of which waited for: 3 -> 3; matrix products, arithmetic and copies ran while one was open for 44% -> 37% of each run, Pallas kernels for 0% -> 0%
where the time goes in v1:
time: 832 us; the launch traced here: 824 us
  local copies, waits for them, and re-layouts  248 us (30%)
  waiting for transfers between devices  244 us (29%)
  matrix products  211 us (25%)
  other arithmetic  77.8 us (9%)
  starting transfers between devices  28.6 us (3%)
  between operations  14.8 us (2%)
    unnamed x2, waiting for transfers between devices  214 us
    reshape x2, local copies, waits for them, and re-layouts, fold_table(): grid = pairs.reshape(heads, span, span, span, span, span, span)  79.5 us
    unnamed x63, local copies, waits for them, and re-layouts  79.1 us
    dot_general x1, matrix products, expand_table(): section = jnp.einsum('hxbcBC,aAx->habcABC', section, ones, precision=exact)  71.1 us
    ppermute x6, waiting for transfers between devices, shifted(): return lax.ppermute(block, axis, route)  29.2 us
    ppermute x6, starting transfers between devices, shifted(): return lax.ppermute(block, axis, route)  28.5 us
    sub x4, matrix products, window_pass(): expo = jnp.exp(scores - top)  27.8 us
    dot_general x4, matrix products, window_pass(): jnp.einsum('ghid,ghjd->ghij', grad_heads, values, preferred_element_type=...  27.7 us
  transfers between devices with their start and end apart: 7, of which 3 were waited for; matrix products, arithmetic and copies ran while one was open for 37% of the time, Pallas kernels for 0%

profile of v1, /device:TPU:1, one launch (start us, length us, event | category | flops | bytes accessed | tf_op | source)
XLA Modules:
  0.0 823.8 jit_solution(8904188467669235827)
XLA Ops:
  7.2 2.4 convert_reduce_fusion
  15.1 3.6 collective-permute-start
  20.4 9.5 %convolution_bitcast_fusion.5 = f32[3,13,7,7,7,7]{1,2,5,3,0,4:T(8,128)S(1)} fusion(f32[3,13,13,7,7]{2,3,1,0,4:T(8,128)S(1)} %convolution_bitcast_fusion.7, s32[7,7]{0,1:T(8,128)S(1)} %subtract_add_fusion), kind=kOutput, calls=%fused_computation.96 | convolution fusion | flops 14608321 | bytes 474124 | tf_op jit(solution)/shard_map/hxycC,bBy->hxbcBC/dot_general | solution.py:44
  30.9 18.6 %collective-permute-start.1 = (bf16[2,28,3,7,96]{4,3,2,1,0:T(8,128)(2,1)S(1)}, bf16[2,28,3,7,96]{4,3,2,1,0:T(8,128)(2,1)S(1)}, u32[]{:S(2)}, u32[]{:S(2)}) collective-permute-start(bf16[2,28,3,7,96]{4,3,2,1,0:T(8,128)(2,1)S(1)} %pad_maximum_fusion.5), channel_id=1, source_target_pairs={{8,0},{16,8},{24,16},{0,24},{9,1},{17,9},{25,17},{1,25},{10,2},{18... | collective-permute-start | bytes 677384 | tf_op jit(solution)/shard_map/ppermute | solution.py:13
  50.3 5.2 collective-permute-done.1
  56.4 2.9 copy.74
  59.3 5.9 collective-permute-start.2
  65.2 71.1 %convolution_bitcast_fusion.3 = f32[3,7,7,7,7,7,7]{6,4,5,3,2,0,1:T(8,128)} fusion(f32[3,13,7,7,7,7]{1,2,5,3,0,4:T(8,128)S(1)} %convolution_bitcast_fusion.5, pred[7,7,13,1,1,1,1]{2,0,1,6,5,4,3:T(8,128)(4,1)S(1)} %fusion.73), kind=kOutput, calls=%fused_computation.61 | convolution fusion | flops 55059736 | bytes 1786981 | tf_op jit(solution)/shard_map/hxbcBC,aAx->habcABC/dot_general | solution.py:45
  137.5 59.5 %copy.82 = f32[3,7,7,7,7,7,7]{3,2,1,6,5,4,0:T(8,128)} copy(f32[3,7,7,7,7,7,7]{6,4,5,3,2,0,1:T(8,128)} %convolution_bitcast_fusion.3) | data formatting | bytes 2823576
  197.0 21.0 %add.230 = f32[3,343,343]{1,2,0:T(8,128)} reshape(f32[3,7,7,7,7,7,7]{3,2,1,6,5,4,0:T(8,128)} %copy.82) | data formatting | bytes 2823576 | tf_op jit(solution)/shard_map/while/body/eval_jaxpr/add | solution.py:127
  225.3 2.5 copy.81
  229.8 2.5 copy.83
  232.3 133.9 %while.20 = (s32[]{:T(128)}, f32[96,288]{1,0:T(8,128)}, f32[288]{0:T(512)S(1)}, f32[96,96]{1,0:T(8,128)S(1)}, f32[3,343,343]{1,2,0:T(8,128)}, /*index=5*/f32[4,4...) while((s32[]{:T(128)}, f32[96,288]{1,0:T(8,128)}, ...), condition=%wide.wide.region_8.9_spmd.clone, body=%wide.wide.region_2.8_spmd.clone.sunk | while | flops 848489408 | bytes 107633568 | solution.py:197
  234.9 6.9 fusion.174
  242.1 6.9 multiply_reduce_fusion.4
  249.0 4.2 fusion.176
  261.0 3.6 fusion.182
  267.2 6.9 fusion.174
  274.4 6.9 multiply_reduce_fusion.4
  281.4 4.2 fusion.176
  292.1 2.7 select_add_fusion.7
  294.8 3.6 fusion.182
  301.0 6.9 fusion.174
  308.2 6.9 multiply_reduce_fusion.4
  315.2 4.2 fusion.176
  325.9 2.7 select_add_fusion.7
  328.6 3.6 fusion.182
  334.8 6.9 fusion.174
  342.0 6.9 multiply_reduce_fusion.4
  349.0 4.2 fusion.176
  359.7 2.7 select_add_fusion.7
  362.4 3.6 fusion.182
  366.2 3.4 copy.84
  372.5 3.5 slice.104
  376.0 19.8 %reshape.174 = f32[3,7,7,7,7,7,7]{3,2,1,6,5,4,0:T(8,128)} reshape(f32[3,343,343]{1,2,0:T(8,128)S(1)} %copy-done) | data formatting | bytes 2823576 | tf_op jit(solution)/shard_map/reshape | solution.py:53
  395.9 59.7 %copy.88 = f32[3,7,7,7,7,7,7]{1,6,4,5,3,2,0:T(8,128)} copy(f32[3,7,7,7,7,7,7]{3,2,1,6,5,4,0:T(8,128)} %reshape.174) | data formatting | bytes 2823576 | tf_op jit(solution)/shard_map/reshape | solution.py:53
  456.3 25.1 %convolution_bitcast_fusion.4 = f32[3,13,7,7,7,7]{1,5,4,3,2,0:T(8,128)} fusion(f32[3,7,7,7,7,7,7]{1,6,4,5,3,2,0:T(8,128)} %copy.88, s32[7,7]{0,1:T(8,128)S(1)} %copy-done.27), kind=kOutput, calls=%fused_computation.95 | convolution fusion | flops 55060372 | bytes 1786540 | tf_op jit(solution)/shard_map/habcABC,aAx->hxbcBC/dot_general | solution.py:54
  481.4 12.6 %copy.89 = f32[3,13,7,7,7,7]{2,3,4,5,1,0:T(8,128)} copy(f32[3,13,7,7,7,7]{1,5,4,3,2,0:T(8,128)} %convolution_bitcast_fusion.4) | data formatting | bytes 749112 | tf_op jit(solution)/shard_map/habcABC,aAx->hxbcBC/transpose | solution.py:54
  499.0 5.4 convolution_bitcast_fusion.6
  506.0 2.9 slice_reduce_fusion
  508.8 24.0 %collective-permute-done.5 = f32[28,28,3,96]{3,1,2,0:T(8,128)} collective-permute-done((f32[28,28,3,96]{3,1,2,0:T(8,128)}, f32[28,28,3,96]{3,1,2,0:T(8,128)}, u32[]{:S(2)}, u32[]{:S(2)}) %collective-permute-start.5) | collective-permute-done | bytes 903200 | tf_op jit(solution)/shard_map/ppermute | solution.py:13
  537.0 5.0 fusion.61
  542.1 7.7 broadcast.244
  549.8 2.5 dynamic-update-slice
  554.6 8.2 fusion.60
  562.8 214.3 %all-reduce.3.cloned.1.call-done = f32[5623680]{0:T(1024)} async-done(((f32[5623680]{0:T(1024)}), f32[5623680]{0:T(1024)}) %all-reduce.3.cloned.1.call-update) | async-done | bytes 22494736
  777.2 27.6 %reshape.175 = f32[128,43935]{1,0:T(8,128)} reshape(f32[5623680]{0:T(1024)} %all-reduce.3.cloned.1.call-done) | data formatting | bytes 44989440 | tf_op jit(solution)/shard_map/all_gather | solution.py:22
  804.8 8.5 %reduce_sum.117 = f32[43935]{0:T(1024)S(1)} reduce(f32[128,43935]{1,0:T(8,128)} %reshape.175, f32[]{:T(128)} %constant.33.clone.1), dimensions={0}, to_apply=%region_14.15 | reduce | flops 5579745 | bytes 22670464 | tf_op jit(solution)/shard_map/reduce_sum | solution.py:23
  (232 shorter events, 78.3 us)
Async XLA Ops:
  7.2 4.6 copy-start.30
  7.2 4.6 copy-start.32
  7.2 770.0 %all-reduce.3.cloned.1.call-start = ((), (), s32[]{:S(2)}) async-start(), calls=%async_computation | async-start | bytes 44990464
  9.8 4.1 copy-start.17
  9.8 5.2 copy-start.5
  13.8 4.9 copy-start.29
  15.1 15.7 %collective-permute-start = (bf16[2,3,28,7,96]{4,3,2,1,0:T(8,128)(2,1)S(1)}, bf16[2,3,28,7,96]{4,3,2,1,0:T(8,128)(2,1)S(1)}, u32[]{:S(2)}, u32[]{:S(2)}) collective-permute-start(bf16[2,3,28,7,96]{4,3,2,1,0:T(8,128)(2,1)S(1)} %pad_maximum_fusion.6), channel_id=1, source_target_pairs={{32,0},{64,32},{96,64},{0,96},{33,1},{65,33},{97,65},{1,97},{34,2}... | collective-permute-start | bytes 677384 | tf_op jit(solution)/shard_map/ppermute | solution.py:13
  18.7 30.8 %copy-start.26 = (s32[7,7]{0,1:T(8,128)}, s32[7,7]{0,1:T(8,128)S(1)}, u32[]{:S(2)}) copy-start(s32[7,7]{0,1:T(8,128)S(1)} %subtract_add_fusion) | copy-start | bytes 592
  19.0 11.0 %copy-start.12 = (bf16[1,28,28,7,96]{4,3,2,1,0:T(8,128)(2,1)S(1)}, bf16[1,28,28,7,96]{4,3,2,1,0:T(8,128)(2,1)}, u32[]{:S(2)}) copy-start(bf16[1,28,28,7,96]{4,3,2,1,0:T(8,128)(2,1)} %copy-done.11) | copy-start | bytes 3161092
  30.9 24.6 %collective-permute-start.1 = (bf16[2,28,3,7,96]{4,3,2,1,0:T(8,128)(2,1)S(1)}, bf16[2,28,3,7,96]{4,3,2,1,0:T(8,128)(2,1)S(1)}, u32[]{:S(2)}, u32[]{:S(2)}) collective-permute-start(bf16[2,28,3,7,96]{4,3,2,1,0:T(8,128)(2,1)S(1)} %pad_maximum_fusion.5), channel_id=1, source_target_pairs={{8,0},{16,8},{24,16},{0,24},{9,1},{17,9},{25,17},{1,25},{10,2},{18... | collective-permute-start | bytes 677384 | tf_op jit(solution)/shard_map/ppermute | solution.py:13
  55.5 3.7 copy-start.23
  59.3 160.4 %collective-permute-start.2 = (bf16[2,28,28,3,96]{4,0,3,2,1:T(2,128)(2,1)}, bf16[2,28,28,3,96]{4,0,3,2,1:T(2,128)(2,1)}, u32[]{:S(2)}, u32[]{:S(2)}) collective-permute-start(bf16[2,28,28,3,96]{4,0,3,2,1:T(2,128)(2,1)} %copy.74), channel_id=1, source_target_pairs={{1,0},{2,1},{3,2},{4,3},{5,4},{6,5},{7,6},{0,7},{9,8},{10,9},{11,1... | collective-permute-start | bytes 2709512 | tf_op jit(solution)/shard_map/ppermute | solution.py:13
  197.0 21.0 %copy-start.24 = (bf16[2,28,3,7,96]{4,3,2,1,0:T(8,128)(2,1)S(1)}, bf16[2,28,3,7,96]{4,3,2,1,0:T(8,128)(2,1)}, u32[]{:S(2)}) copy-start(bf16[2,28,3,7,96]{4,3,2,1,0:T(8,128)(2,1)} %copy-done.23) | copy-start | bytes 677380
  227.9 4.4 copy-start.19
  227.9 4.4 copy-start.25
  227.9 4.4 copy-start.28
  232.5 9.3 %copy-start.9 = (bf16[4,4,343,96]{2,3,1,0:T(8,128)(2,1)}, bf16[4,4,343,96]{2,3,1,0:T(8,128)(2,1)S(1)}, u32[]{:S(2)}) copy-start(bf16[4,4,343,96]{2,3,1,0:T(8,128)(2,1)S(1)} %get-tuple-element.413) | copy-start | bytes 3161092 | tf_op jit(solution)/shard_map/while
  232.5 9.3 %copy-start.13 = (bf16[4,4,343,96]{2,3,1,0:T(8,128)(2,1)}, bf16[4,4,343,96]{2,3,1,0:T(8,128)(2,1)S(1)}, u32[]{:S(2)}) copy-start(bf16[4,4,343,96]{2,3,1,0:T(8,128)(2,1)S(1)} %get-tuple-element.418) | copy-start | bytes 3161092 | tf_op jit(solution)/shard_map/while
  242.1 6.9 slice-start
  242.1 6.9 slice-start.1
  261.0 3.8 copy-start.10
  264.8 9.3 %copy-start.9 = (bf16[4,4,343,96]{2,3,1,0:T(8,128)(2,1)}, bf16[4,4,343,96]{2,3,1,0:T(8,128)(2,1)S(1)}, u32[]{:S(2)}) copy-start(bf16[4,4,343,96]{2,3,1,0:T(8,128)(2,1)S(1)} %get-tuple-element.413) | copy-start | bytes 3161092 | tf_op jit(solution)/shard_map/while
  264.9 9.3 %copy-start.13 = (bf16[4,4,343,96]{2,3,1,0:T(8,128)(2,1)}, bf16[4,4,343,96]{2,3,1,0:T(8,128)(2,1)S(1)}, u32[]{:S(2)}) copy-start(bf16[4,4,343,96]{2,3,1,0:T(8,128)(2,1)S(1)} %get-tuple-element.418) | copy-start | bytes 3161092 | tf_op jit(solution)/shard_map/while
  274.4 6.9 slice-start
  274.4 6.9 slice-start.1
  294.8 3.8 copy-start.10
  298.6 9.3 %copy-start.9 = (bf16[4,4,343,96]{2,3,1,0:T(8,128)(2,1)}, bf16[4,4,343,96]{2,3,1,0:T(8,128)(2,1)S(1)}, u32[]{:S(2)}) copy-start(bf16[4,4,343,96]{2,3,1,0:T(8,128)(2,1)S(1)} %get-tuple-element.413) | copy-start | bytes 3161092 | tf_op jit(solution)/shard_map/while
  298.7 9.3 %copy-start.13 = (bf16[4,4,343,96]{2,3,1,0:T(8,128)(2,1)}, bf16[4,4,343,96]{2,3,1,0:T(8,128)(2,1)S(1)}, u32[]{:S(2)}) copy-start(bf16[4,4,343,96]{2,3,1,0:T(8,128)(2,1)S(1)} %get-tuple-element.418) | copy-start | bytes 3161092 | tf_op jit(solution)/shard_map/while
  308.2 6.9 slice-start
  308.2 6.9 slice-start.1
  328.6 3.8 copy-start.10
  332.5 9.3 %copy-start.9 = (bf16[4,4,343,96]{2,3,1,0:T(8,128)(2,1)}, bf16[4,4,343,96]{2,3,1,0:T(8,128)(2,1)S(1)}, u32[]{:S(2)}) copy-start(bf16[4,4,343,96]{2,3,1,0:T(8,128)(2,1)S(1)} %get-tuple-element.413) | copy-start | bytes 3161092 | tf_op jit(solution)/shard_map/while
  332.5 9.3 %copy-start.13 = (bf16[4,4,343,96]{2,3,1,0:T(8,128)(2,1)}, bf16[4,4,343,96]{2,3,1,0:T(8,128)(2,1)S(1)}, u32[]{:S(2)}) copy-start(bf16[4,4,343,96]{2,3,1,0:T(8,128)(2,1)S(1)} %get-tuple-element.418) | copy-start | bytes 3161092 | tf_op jit(solution)/shard_map/while
  342.0 6.9 slice-start
  342.0 6.9 slice-start.1
  362.4 3.8 copy-start.10
  371.7 4.3 copy-start
  372.5 83.1 %collective-permute-start.3 = (f32[3,28,7,96]{3,2,1,0:T(8,128)}, f32[3,28,7,96]{3,2,1,0:T(8,128)S(1)}, u32[]{:S(2)}, u32[]{:S(2)}) collective-permute-start(f32[3,28,7,96]{3,2,1,0:T(8,128)} %slice.103), channel_id=1, source_target_pairs={{96,0},{0,32},{32,64},{64,96},{97,1},{1,33},{33,65},{65,97},{98,2}... | collective-permute-start | bytes 677384 | tf_op jit(solution)/shard_map/ppermute | solution.py:13
  395.9 59.7 %copy-start.4 = (f32[25,28,7,96]{3,2,1,0:T(8,128)S(1)}, f32[25,28,7,96]{3,2,1,0:T(8,128)}, u32[]{:S(2)}) copy-start(f32[25,28,7,96]{3,2,1,0:T(8,128)} %slice.104) | copy-start | bytes 5644804
  456.3 37.7 %collective-permute-start.4 = (f32[28,3,7,96]{3,2,1,0:T(8,128)}, f32[28,3,7,96]{3,2,1,0:T(8,128)}, u32[]{:S(2)}, u32[]{:S(2)}) collective-permute-start(f32[28,3,7,96]{3,2,1,0:T(8,128)} %pad_maximum_fusion.4), channel_id=1, source_target_pairs={{24,0},{0,8},{8,16},{16,24},{25,1},{1,9},{9,17},{17,25},{26,2},{2,... | collective-permute-start | bytes 677384 | tf_op jit(solution)/shard_map/ppermute | solution.py:13
  494.0 5.0 copy-start.3
  495.6 8.8 %copy-start.15 = (f32[28,28,7,96]{3,2,1,0:T(8,128)}, f32[28,28,7,96]{3,2,1,0:T(8,128)S(1)}, u32[]{:S(2)}) copy-start(f32[28,28,7,96]{3,2,1,0:T(8,128)S(1)} %fusion.63) | copy-start | bytes 6322180
  497.3 8.4 %copy-start.22 = (f32[96,288]{1,0:T(8,128)S(1)}, f32[96,288]{1,0:T(8,128)}, u32[]{:S(2)}) copy-start(f32[96,288]{1,0:T(8,128)} %get-tuple-element.79) | copy-start | bytes 331780
  497.3 35.6 %collective-permute-start.5 = (f32[28,28,3,96]{3,1,2,0:T(8,128)}, f32[28,28,3,96]{3,1,2,0:T(8,128)}, u32[]{:S(2)}, u32[]{:S(2)}) collective-permute-start(f32[28,28,3,96]{3,1,2,0:T(8,128)} %copy.86), channel_id=1, source_target_pairs={{7,0},{0,1},{1,2},{2,3},{3,4},{4,5},{5,6},{6,7},{15,8},{8,9},{9,10... | collective-permute-start | bytes 2709512 | tf_op jit(solution)/shard_map/ppermute | solution.py:13
  505.9 31.0 %copy-start.2 = (bf16[28,28,7,96]{3,2,1,0:T(8,128)(2,1)S(1)}, bf16[28,28,7,96]{3,2,1,0:T(8,128)(2,1)}, u32[]{:S(2)}) copy-start(bf16[28,28,7,96]{3,2,1,0:T(8,128)(2,1)} %param.10) | copy-start | bytes 3161092
  506.0 31.0 %copy-start.31 = (f32[96]{0:T(128)S(1)}, f32[96]{0:T(128)}, u32[]{:S(2)}) copy-start(f32[96]{0:T(128)} %param.12) | copy-start | bytes 1156
  508.8 33.1 %copy-start.7 = (f32[28,28,4,96]{3,2,1,0:T(4,128)}, f32[28,28,4,96]{3,2,1,0:T(4,128)S(1)}, u32[]{:S(2)}) copy-start(f32[28,28,4,96]{3,2,1,0:T(4,128)S(1)} %get-tuple-element.213) | copy-start | bytes 3612676
  536.9 5.0 copy-start.8
  (12 other events, 30.9 us)
Sparse Core Ops, SparseCore 0:
  552.5 224.6 all-reduce.2
